TPU v7x, 32 devices: a whole 2x2x4 slice. The times are simulated.
32 devices in a mesh: samples: 4 (over y, x), channel: 4 (over z), spatial: 2 (over core).
Axes of the slice: x: 2, y: 2, z: 4, core: 2. Of those that a mesh axis runs over, the one named last changes fastest.
Arguments:
- features: bfloat16 [512, 4, 2, 1024], P('channel', 'samples', 'spatial'), may hold values from -6 to 6
- conv_one: bfloat16 [27, 512, 512], P(None, 'channel'), may hold values from -0.0625 to 0.0625
- conv_two: bfloat16 [27, 512, 512], P(None, 'channel'), may hold values from -0.0625 to 0.0625
- cotangent: bfloat16 [512, 4, 2, 1024], P('channel', 'samples', 'spatial'), may hold values from -6 to 6
Outputs:
- mixed_out: bfloat16 [512, 4, 2, 1024], P('channel', 'samples', 'spatial')
- input_grad: bfloat16 [512, 4, 2, 1024], P('channel', 'samples', 'spatial')
- grad_one: float32 [27, 512, 512], P(None, 'channel')
- grad_two: float32 [27, 512, 512], P(None, 'channel')
All inputs are finite; a program needn't handle non-finite values.
Results may differ from a plain program's by a relative error of at most 0.017.
Values may be sent and summed in bfloat16 or wider, within the bound.
A program may use at most 128 MiB of HBM per device.

v0:
```python
import jax
import jax.numpy as jnp
from jax import lax
from jax.sharding import PartitionSpec as P

SIDE = 32


def with_halo(shard, sides, width):
    for axis, dim in sides:
        size, length = (lax.axis_size(axis), shard.shape[dim])
        up = [(i, (i + 1) % size) for i in range(size - 1)]
        down = [(j, i) for i, j in up]
        last = lax.slice_in_dim(shard, length - width, length, axis=dim)
        first = lax.slice_in_dim(shard, 0, width, axis=dim)
        before = lax.ppermute(last, axis, up)
        after = lax.ppermute(first, axis, down)
        shard = jnp.concatenate([before, shard, after], axis=dim)
    return shard


def to_grid(values):
    return values.reshape(values.shape[0], values.shape[1], values.shape[2], SIDE, SIDE)


def to_flat(values):
    return values.reshape(values.shape[0], values.shape[1], values.shape[2], SIDE * SIDE)


def as_taps(kernel):
    return kernel.reshape(3, 3, 3, kernel.shape[1], kernel.shape[2])


def forward_conv(source, kernel, rhs_spec):
    return lax.conv_general_dilated(
        source,
        as_taps(kernel),
        (1, 1, 1),
        [(0, 0), (1, 1), (1, 1)],
        dimension_numbers=("CNDHW", rhs_spec, "CNDHW"),
        preferred_element_type=jnp.float32,
    )


def data_grad(source, kernel, rhs_spec):
    flipped = as_taps(kernel)[::-1, ::-1, ::-1]
    return lax.conv_general_dilated(
        source,
        flipped,
        (1, 1, 1),
        [(0, 0), (1, 1), (1, 1)],
        dimension_numbers=("CNDHW", rhs_spec, "CNDHW"),
        preferred_element_type=jnp.float32,
    )


def weight_grad(padded, upstream, out_spec):
    result = lax.conv_general_dilated(
        padded,
        upstream,
        (1, 1, 1),
        [(0, 0), (0, 0), (0, 0)],
        dimension_numbers=("NCDHW", "OIDHW", out_spec),
        preferred_element_type=jnp.float32,
    )
    return result.reshape(27, result.shape[3], result.shape[4])


def pad_plane(values):
    return jnp.pad(values, ((0, 0), (0, 0), (0, 0), (1, 1), (1, 1)))


def body(features, conv_one, conv_two, cotangent):
    rims_x = with_halo(features, (("spatial", 2),), 1)
    whole_x = lax.all_gather(rims_x, "channel", axis=0, tiled=True)
    pre_act = forward_conv(to_grid(whole_x), conv_one, "DHWOI")
    hidden = jax.nn.silu(pre_act).astype(jnp.bfloat16)
    rims_h = with_halo(to_flat(hidden), (("spatial", 2),), 1)
    grid_h = to_grid(rims_h)
    weight_part = conv_two
    mixed_out = lax.psum_scatter(
        to_flat(forward_conv(grid_h, weight_part, "DHWIO")),
        "channel",
        scatter_dimension=0,
        tiled=True,
    ).astype(jnp.bfloat16)
    rims_c = with_halo(cotangent, (("spatial", 2),), 1)
    whole_c = to_grid(lax.all_gather(rims_c, "channel", axis=0, tiled=True))
    hidden_grad = data_grad(whole_c, conv_two, "DHWOI")
    sigmoid_v = jax.nn.sigmoid(pre_act)
    act_grad = (hidden_grad * sigmoid_v * (1.0 + pre_act * (1.0 - sigmoid_v))).astype(jnp.bfloat16)
    rims_g = with_halo(to_flat(act_grad), (("spatial", 2),), 1)
    grid_g = to_grid(rims_g)
    weight_part = conv_one
    input_grad = lax.psum_scatter(
        to_flat(data_grad(grid_g, weight_part, "DHWIO")).astype(jnp.bfloat16),
        "channel",
        scatter_dimension=0,
        tiled=True,
    )
    local_two = weight_grad(pad_plane(grid_h), whole_c[:, :, 1:-1], "DHWNC")
    local_one = weight_grad(pad_plane(to_grid(whole_x)), act_grad, "DHWCN")
    grad_one, grad_two = (
        lax.psum(local_one.astype(jnp.bfloat16), ("samples", "spatial")).astype(jnp.float32),
        lax.psum(local_two.astype(jnp.bfloat16), ("samples", "spatial")).astype(jnp.float32),
    )
    return (mixed_out, input_grad, grad_one, grad_two)


def solution(mesh):
    placed = (
        P("channel", "samples", "spatial", None),
        P(None, "channel", None),
        P(None, "channel", None),
        P("channel", "samples", "spatial", None),
    )
    return jax.shard_map(
        body,
        mesh=mesh,
        in_specs=placed,
        out_specs=(
            P("channel", "samples", "spatial", None),
            P("channel", "samples", "spatial", None),
            P(None, "channel", None),
            P(None, "channel", None),
        ),
        check_vma=False,
    )
```

profile of v0, /device:TPU:0, one launch (start us, length us, event | category | flops | bytes accessed | tf_op | source)
XLA Modules:
  0.0 412.4 jit_solution(8968176364339753036)
XLA Ops:
  7.2 1.9 copy.91
  9.2 2.4 collective-permute-start
  11.6 1.3 collective-permute-start.1
  12.9 2.3 collective-permute-done.1
  15.2 1.9 pad_maximum_fusion.1
  17.2 1.8 copy.106
  19.0 2.0 collective-permute-start.4
  21.1 1.3 collective-permute-start.5
  22.4 2.3 collective-permute-done.5
  24.7 1.9 pad_maximum_fusion.2
  26.7 56.1 %all-gather.3.cloned.1.call-done = bf16[512,1,3,1024]{0,3,2,1:T(8,128)(2,1)} async-done(((bf16[128,1,3,1024]{0,3,2,1:T(8,128)(2,1)}), bf16[512,1,3,1024]{0,3,2,1:T(8,128)(2,1)}) %all-gather.3.cloned.1.call-update) | async-done | bytes 3145744 | tf_op jit(solution)/shard_map/all_gather | solution.py:75
  82.8 3.6 copy.144
  86.4 1.3 fusion.85
  87.8 2.2 copy.96
  90.4 10.3 %multiply_convert_fusion = (bf16[1,32,8,5,128]{4,2,3,1,0:T(8,128)(2,1)S(1)}, f32[1,32,8,5,128]{4,2,3,1,0:T(8,128)}) fusion(bf16[3,3,3,128,512]{4,3,2,1,0:T(8,128)(2,1)S(1)} %bitcast.81, bf16[512,3,32,1,7,2]{0,4,5,2,1,3:T(8,128)(2,1)S(1)} %slice.16, bf16[512,3,32,1,8,5]{0,4,5,2,1,3:T(8,128)(2,1)S(1)} %copy.96, pred[8,5]{0,1:T(8,128)(4,1)S(1)} %copy-done.15), kind=kOutput, calls=%fused_computation.63 | convolution fusion | flops 4452974592 | bytes 9830440 | tf_op jit(solution)/shard_map/conv_general_dilated | solution.py:35
  102.9 1.3 collective-permute-start.3
  104.2 4.7 %collective-permute-start.2 = (bf16[128,1,1,1024]{0,3,2,1:T(8,128)(2,1)}, bf16[128,1,1,1024]{0,3,2,1:T(8,128)(2,1)}, u32[]{:S(2)}, u32[]{:S(2)}) collective-permute-start(bf16[128,1,1,1024]{0,3,2,1:T(8,128)(2,1)} %bitcast.42), channel_id=1, source_target_pairs={{0,1},{2,3},{4,5},{6,7},{8,9},{10,11},{12,13},{14,15},{16,17},{18,... | collective-permute-start | bytes 786440 | tf_op jit(solution)/shard_map/ppermute | solution.py:16
  108.8 1.3 fusion.84
  110.1 3.5 fusion.83
  113.6 32.3 %all-gather.5.cloned.1.call-done = bf16[512,1,3,1024]{0,3,2,1:T(8,128)(2,1)} async-done(((bf16[128,1,3,1024]{0,3,2,1:T(8,128)(2,1)}), bf16[512,1,3,1024]{0,3,2,1:T(8,128)(2,1)}) %all-gather.5.cloned.1.call-update) | async-done | bytes 3145744 | tf_op jit(solution)/shard_map/all_gather | solution.py:88
  145.9 3.6 copy.147
  150.2 2.2 copy.111
  152.9 9.9 %fusion.57 = bf16[1,32,8,5,128]{4,2,3,1,0:T(8,128)(2,1)S(1)} fusion(bf16[3,3,3,128,512]{4,3,2,1,0:T(8,128)(2,1)S(1)} %bitcast.105, bf16[512,3,32,1,7,2]{0,4,5,2,1,3:T(8,128)(2,1)S(1)} %slice.20, bf16[512,3,32,1,8,5]{0,4,5,2,1,3:T(8,128)(2,1)S(1)} %copy.111, f32[1,32,8,5,128]{4,2,3,1,0:T(8,128)S(1)} %copy-done.17, pred[8,5]{0,1:T(8,128)(4,1)S(1)} %copy-done.15), kind=kOutput, calls=%fused_computation.54 | convolution fusion | flops 4453629952 | bytes 9830440 | tf_op jit(solution)/shard_map/conv_general_dilated | solution.py:47
  163.7 2.1 collective-permute-start.6
  165.9 1.3 collective-permute-start.7
  167.2 1.8 copy.140
  169.0 1.8 copy.141
  171.6 2.2 copy.126
  173.8 1.2 fusion.25
  175.1 15.5 %fusion.32 = bf16[3,3,3,128,512,1]{3,4,2,5,1,0:T(8,128)(2,1)} fusion(bf16[512,3,32,8,5,1]{0,3,5,4,2,1:T(8,128)(2,1)S(1)} %get-tuple-element.26, bf16[512,3,32,8,5,1]{0,3,5,4,2,1:T(8,128)(2,1)S(1)} %copy.126, bf16[512,3,32,8,5,1]{0,3,5,4,2,1:T(8,128)(2,1)S(1)} %get-tuple-element.27, bf16[1,32,8,5,128]{4,2,3,1,0:T(8,128)(2,1)S(1)} %fusion.57, ...), kind=kOutput, calls=%fused_computation.36 | convolution fusion | flops 4472799232 | bytes 15663144 | tf_op jit(solution)/shard_map/conv_general_dilated | solution.py:58
  190.6 5.9 %copy.128 = bf16[27,128,512]{2,1,0:T(8,128)(2,1)} copy(bf16[27,128,512]{1,2,0:T(8,128)(2,1)} %bitcast.99) | data formatting | bytes 7077888 | tf_op jit(solution)/shard_map/convert_element_type | solution.py:104
  196.5 2.4 slice.28
  198.9 2.3 copy.100
  201.2 2.3 copy.99
  206.3 4.9 %select_convert_fusion = bf16[1,32,8,5,512]{4,2,3,1,0:T(8,128)(2,1)S(1)} fusion(bf16[3,3,3,128,512]{4,3,2,1,0:T(8,128)(2,1)S(1)} %bitcast.82, bf16[128,3,32,1,7,2]{0,4,5,2,1,3:T(8,128)(2,1)S(1)} %slice.22, bf16[128,3,32,1,8,5]{0,4,5,2,1,3:T(8,128)(2,1)S(1)} %copy.117, pred[8,5]{0,1:T(8,128)(4,1)S(1)} %copy-done.15), kind=kOutput, calls=%fused_computation.34 | convolution fusion | flops 4440915968 | bytes 6176808 | tf_op jit(solution)/shard_map/conv_general_dilated | solution.py:47
  212.4 1.3 copy.134
  213.8 4.6 %pad_maximum_fusion = bf16[128,1,3,32,32]{0,1,4,3,2:T(2,128)(2,1)S(1)} fusion(bf16[128,1,1,32,32]{0,1,4,3,2:T(2,128)(2,1)} %copy.100, bf16[128,1,1,32,32]{0,1,4,3,2:T(2,128)(2,1)S(1)} %bitcast.93, bf16[128,1,1,32,32]{0,1,4,3,2:T(2,128)(2,1)} %copy.99), kind=kLoop, calls=%fused_computation.40 | loop fusion | flops 786432 | bytes 1572864 | tf_op jit(solution)/shard_map/concatenate | solution.py:18
  218.4 20.4 %convolution_convert_fusion = bf16[3,3,3,128,512]{4,3,2,1,0:T(8,128)(2,1)} fusion(bf16[128,1,3,32,32]{0,1,4,3,2:T(2,128)(2,1)S(1)} %pad_maximum_fusion, bf16[512,1,1,32,32]{0,4,3,2,1:T(8,128)(2,1)} %slice.28), kind=kOutput, calls=%fused_computation.35 | convolution fusion | flops 3476226048 | bytes 5373952 | tf_op jit(solution)/shard_map/conv_general_dilated | solution.py:58
  241.1 5.0 %convolution_select_fusion = f32[1,32,8,5,512]{4,2,3,1,0:T(8,128)S(1)} fusion(bf16[3,3,3,128,512]{4,3,2,1,0:T(8,128)(2,1)S(1)} %bitcast.106, bf16[128,3,32,1,7,2]{0,4,5,2,1,3:T(8,128)(2,1)S(1)} %slice.18, bf16[128,3,32,1,8,5]{0,4,5,2,1,3:T(8,128)(2,1)S(1)} %copy.103, pred[8,5]{0,1:T(8,128)(4,1)S(1)} %copy-done.16), kind=kOutput, calls=%fused_computation.39 | convolution fusion | flops 4440260608 | bytes 7487528 | tf_op jit(solution)/shard_map/conv_general_dilated | solution.py:35
  246.0 1.5 copy.104
  247.8 2.6 copy.105
  250.4 1.1 copy.135
  252.4 103.8 %all-reduce.3.cloned.1.call-done = (bf16[27,128,512]{2,1,0:T(8,128)(2,1)}, bf16[27,128,512]{2,1,0:T(8,128)(2,1)}) async-done(((bf16[27,128,512]{2,1,0:T(8,128)(2,1)}, bf16[27,128,512]{2,1,0:T(8,128)(2,1)}), (bf16[27,128,512]{2,1,0:T(8,128)(2,1)}, bf16[27,128,512]{2,1,0:T(8,128)(2,1)})) %all-reduce.3.cloned.1.call-update) | async-done | bytes 7077904 | tf_op jit(solution)/shard_map/psum | solution.py:104
  356.2 6.1 %convert_element_type.52 = f32[27,128,512]{2,1,0:T(8,128)} convert(bf16[27,128,512]{2,1,0:T(8,128)(2,1)} %get-tuple-element.16) | non-fusion elementwise | flops 1769472 | bytes 10616832 | tf_op jit(solution)/shard_map/convert_element_type | solution.py:104
  362.3 4.0 convert_element_type.55
  366.3 35.9 %reduce-scatter.5.cloned.1.call-done = f32[128,1,1,1024]{0,3,2,1:T(8,128)} async-done(((f32[512,1,1,1024]{0,3,2,1:T(8,128)}), f32[128,1,1,1024]{0,3,2,1:T(8,128)}) %reduce-scatter.5.cloned.1.call-update) | async-done | bytes 524304 | tf_op jit(solution)/shard_map/reduce_scatter | solution.py:81
  402.1 1.8 convert_element_type.46
  403.9 1.8 copy.130
  (81 shorter events, 12.6 us)
Async XLA Ops:
  7.2 83.2 %copy-start = (bf16[27,128,512]{2,1,0:T(8,128)(2,1)S(1)}, bf16[27,128,512]{2,1,0:T(8,128)(2,1)}, u32[]{:S(2)}) copy-start(bf16[27,128,512]{2,1,0:T(8,128)(2,1)} %param.5) | copy-start | bytes 10616836
  7.2 75.6 %all-gather.3.cloned.1.call-start = ((), (), s32[]{:S(2)}) async-start(), calls=%async_computation.2 | async-start | bytes 3932160 | tf_op jit(solution)/shard_map/all_gather | solution.py:75
  9.2 3.7 collective-permute-start
  11.6 3.6 collective-permute-start.1
  17.2 128.8 %all-gather.5.cloned.1.call-start = ((), (), s32[]{:S(2)}) async-start(), calls=%async_computation.4 | async-start | bytes 3932160 | tf_op jit(solution)/shard_map/all_gather | solution.py:88
  19.0 3.4 collective-permute-start.4
  21.1 3.6 collective-permute-start.5
  26.6 223.8 %reduce-scatter.7.cloned.1.call-start = ((), (), s32[]{:S(2)}) async-start(), calls=%async_computation.5 | async-start | bytes 1310720
  87.7 22.4 %copy-start.2 = (bf16[512,3,32,1,40]{0,2,4,1,3:T(8,128)(2,1)}, bf16[512,3,32,1,40]{0,2,4,1,3:T(8,128)(2,1)S(1)}, u32[]{:S(2)}) copy-start(bf16[512,3,32,1,40]{0,2,4,1,3:T(8,128)(2,1)S(1)} %get-tuple-element.22) | copy-start | bytes 11796484
  87.8 2.7 copy-start.15
  101.3 0.8 copy-start.6
  102.9 96.0 %collective-permute-start.3 = (bf16[128,1,1,1024]{0,3,2,1:T(8,128)(2,1)}, bf16[128,1,1,1024]{0,3,2,1:T(8,128)(2,1)}, u32[]{:S(2)}, u32[]{:S(2)}) collective-permute-start(bf16[128,1,1,1024]{0,3,2,1:T(8,128)(2,1)} %bitcast.42), channel_id=1, source_target_pairs={{1,0},{3,2},{5,4},{7,6},{9,8},{11,10},{13,12},{15,14},{17,16},{19,... | collective-permute-start | bytes 786440 | tf_op jit(solution)/shard_map/ppermute | solution.py:17
  104.2 97.0 %collective-permute-start.2 = (bf16[128,1,1,1024]{0,3,2,1:T(8,128)(2,1)}, bf16[128,1,1,1024]{0,3,2,1:T(8,128)(2,1)}, u32[]{:S(2)}, u32[]{:S(2)}) collective-permute-start(bf16[128,1,1,1024]{0,3,2,1:T(8,128)(2,1)} %bitcast.42), channel_id=1, source_target_pairs={{0,1},{2,3},{4,5},{6,7},{8,9},{10,11},{12,13},{14,15},{16,17},{18,... | collective-permute-start | bytes 786440 | tf_op jit(solution)/shard_map/ppermute | solution.py:16
  150.1 2.7 copy-start.13
  150.2 2.7 copy-start.17
  152.9 14.3 %copy-start.5 = (bf16[512,3,32,1,8,4]{0,2,5,4,1,3:T(8,128)(2,1)S(1)}, bf16[512,3,32,1,8,4]{0,2,5,4,1,3:T(8,128)(2,1)}, u32[]{:S(2)}) copy-start(bf16[512,3,32,1,8,4]{0,2,5,4,1,3:T(8,128)(2,1)} %get-tuple-element.18) | copy-start | bytes 9437188
  162.9 4.3 %copy-start.11 = (bf16[128,1,1,32,32]{0,3,4,1,2:T(8,128)(2,1)}, bf16[128,1,1,32,32]{0,3,4,1,2:T(8,128)(2,1)S(1)}, u32[]{:S(2)}) copy-start(bf16[128,1,1,32,32]{0,3,4,1,2:T(8,128)(2,1)S(1)} %slice_bitcast_fusion.2) | copy-start | bytes 786436
  162.9 6.0 %copy-start.4 = (bf16[512,3,32,1,8,4]{0,2,5,4,1,3:T(8,128)(2,1)S(1)}, bf16[512,3,32,1,8,4]{0,2,5,4,1,3:T(8,128)(2,1)}, u32[]{:S(2)}) copy-start(bf16[512,3,32,1,8,4]{0,2,5,4,1,3:T(8,128)(2,1)} %get-tuple-element.19) | copy-start | bytes 9437188
  163.7 39.8 %collective-permute-start.6 = (bf16[128,1,1,1024]{0,3,2,1:T(8,128)(2,1)}, bf16[128,1,1,1024]{0,3,2,1:T(8,128)(2,1)}, u32[]{:S(2)}, u32[]{:S(2)}) collective-permute-start(bf16[128,1,1,1024]{0,3,2,1:T(8,128)(2,1)} %bitcast.20), channel_id=1, source_target_pairs={{0,1},{2,3},{4,5},{6,7},{8,9},{10,11},{12,13},{14,15},{16,17},{18,... | collective-permute-start | bytes 786440 | tf_op jit(solution)/shard_map/ppermute | solution.py:16
  165.9 38.7 %collective-permute-start.7 = (bf16[128,1,1,1024]{0,3,2,1:T(8,128)(2,1)}, bf16[128,1,1,1024]{0,3,2,1:T(8,128)(2,1)}, u32[]{:S(2)}, u32[]{:S(2)}) collective-permute-start(bf16[128,1,1,1024]{0,3,2,1:T(8,128)(2,1)} %bitcast.20), channel_id=1, source_target_pairs={{1,0},{3,2},{5,4},{7,6},{9,8},{11,10},{13,12},{15,14},{17,16},{19,... | collective-permute-start | bytes 786440 | tf_op jit(solution)/shard_map/ppermute | solution.py:17
  168.9 1.8 copy-start.10
  169.0 2.2 copy-start.9
  169.0 2.6 copy-start.3
  196.5 9.2 %copy-start.12 = (bf16[128,1,1,32,32]{0,3,4,1,2:T(8,128)(2,1)S(1)}, bf16[128,1,1,32,32]{0,3,4,1,2:T(8,128)(2,1)}, u32[]{:S(2)}) copy-start(bf16[128,1,1,32,32]{0,3,4,1,2:T(8,128)(2,1)} %copy-done.11) | copy-start | bytes 786436
  211.7 2.1 copy-start.7
  213.7 142.5 %all-reduce.3.cloned.1.call-start = ((), (), s32[]{:S(2)}) async-start(), calls=%async_computation.6 | async-start | bytes 14155776 | tf_op jit(solution)/shard_map/psum | solution.py:104
  238.8 163.3 %reduce-scatter.5.cloned.1.call-start = ((), (), s32[]{:S(2)}) async-start(), calls=%async_computation.3 | async-start | bytes 2621440 | tf_op jit(solution)/shard_map/reduce_scatter | solution.py:81
  239.0 2.0 copy-start.14
  239.1 2.0 copy-start.16
  356.2 6.1 %copy-start.8 = (bf16[27,128,512]{2,1,0:T(8,128)(2,1)S(1)}, bf16[27,128,512]{2,1,0:T(8,128)(2,1)}, u32[]{:S(2)}) copy-start(bf16[27,128,512]{2,1,0:T(8,128)(2,1)} %get-tuple-element.17) | copy-start | bytes 10616836
  362.3 43.4 %copy-start.1 = (bf16[27,128,512]{2,1,0:T(8,128)(2,1)S(1)}, bf16[27,128,512]{2,1,0:T(8,128)(2,1)}, u32[]{:S(2)}) copy-start(bf16[27,128,512]{2,1,0:T(8,128)(2,1)} %param.5) | copy-start | bytes 10616836
Sparse Core Ops, SparseCore 0:
  17.3 65.4 all-gather.2
  84.3 61.5 all-gather.4
  213.9 27.3 reduce-scatter.6
  245.1 111.0 all-reduce.2
  358.3 43.7 reduce-scatter.4
where the time goes:
time: 416 us; the launch traced here: 412 us
  waiting for transfers between devices  233 us (56%)
  matrix products  66 us (16%)
  local copies, waits for them, and re-layouts  60.9 us (15%)
  other arithmetic  21.5 us (5%)
  starting transfers between devices  16.6 us (4%)
  between operations  14.5 us (3%)
    psum x1, waiting for transfers between devices, body(): lax.psum(local_one.astype(jnp.bfloat16), ('samples', 'spatial'))  104 us
    all_gather x1, waiting for transfers between devices, body(): whole_x = lax.all_gather(rims_x, 'channel', axis=0, tiled=True)  56.1 us
    conv_general_dilated x2, matrix products, weight_grad(): lax.conv_general_dilated(padded, upstream, (1, 1, 1), [(0, 0), (0, 0), (0...  35.9 us
    reduce_scatter x1, waiting for transfers between devices, body(): lax.psum_scatter(to_flat(forward_conv(grid_h, weight_part, 'DHWIO')), 'ch...  35.9 us
    all_gather x1, waiting for transfers between devices, body(): whole_c = to_grid(lax.all_gather(rims_c, 'channel', axis=0, tiled=True))  32.3 us
    unnamed x52, local copies, waits for them, and re-layouts  24.2 us
    conv_general_dilated x2, matrix products, forward_conv(): lax.conv_general_dilated(source, as_taps(kernel), (1, 1, 1), [(0, 0), (1,...  15.2 us
    conv_general_dilated x2, matrix products, data_grad(): lax.conv_general_dilated(source, flipped, (1, 1, 1), [(0, 0), (1, 1), (1,...  14.9 us
  transfers between devices with their start and end apart: 13, of which 6 were waited for; matrix products, arithmetic and copies ran while one was open for 32% of the time, Pallas kernels for 0%

commit v1 on v0

v1 whole, which is shorter than its diff:
```python
import functools
import math

import jax
import jax.numpy as jnp
from jax import lax
from jax.experimental import pallas as pl
from jax.experimental.pallas import tpu as pltpu
from jax.sharding import PartitionSpec as P

LANES = 256
ROWS = 16


def shifted(values, dy, dx, side):
    plane = values.shape[1]
    amount = (-(dy * side + dx)) % plane
    if amount == 0:
        return values
    cell = lax.broadcasted_iota(jnp.int32, values.shape, 1)
    row, col = cell // side + dy, cell % side + dx
    inside = (row >= 0) & (row < side) & (col >= 0) & (col < side)
    return jnp.where(inside, pltpu.roll(values, amount, 1), 0.0)


def offsets(sign):
    return [(sign * (b - 1), sign * (c - 1)) for b in range(3) for c in range(3)]


def other_tap(sign):
    s = lax.axis_index("spatial")
    return 2 - 2 * s if sign > 0 else 2 * s


def product_over_channels(sign, side, own_ref, oth_ref, w_ref, y_ref, finish):
    held = w_ref.shape[0] // 27
    plane = own_ref.shape[1]
    third = 9 * held
    away = pl.multiple_of(other_tap(sign) * third, third)

    @pl.loop(0, plane // LANES)
    def _(n):
        cols = pl.ds(pl.multiple_of(n * LANES, LANES), LANES)
        y_ref[:, cols] = jnp.dot(
            w_ref[third : 2 * third, :], own_ref[:, cols], preferred_element_type=jnp.float32
        ) + jnp.dot(
            w_ref[pl.ds(away, third), :], oth_ref[:, cols], preferred_element_type=jnp.float32
        )

    @pl.loop(0, held // ROWS)
    def _(k):
        base = pl.multiple_of(k * ROWS, ROWS)
        total = None
        for t, (dy, dx) in enumerate(offsets(sign)):
            part = shifted(y_ref[pl.ds(base + t * held, ROWS), :], dy, dx, side)
            total = part if total is None else total + part
        finish(pl.ds(base, ROWS), total)


def forward_kernel(side, own_ref, oth_ref, w_ref, pre_ref, hid_ref, y_ref):
    def finish(rows, total):
        pre_ref[rows, :] = total
        hid_ref[rows, :] = (total / (1.0 + jnp.exp(-total))).astype(jnp.bfloat16)

    product_over_channels(1, side, own_ref, oth_ref, w_ref, y_ref, finish)


def backward_kernel(side, own_ref, oth_ref, w_ref, pre_ref, act_ref, y_ref):
    def finish(rows, total):
        pre = pre_ref[rows, :]
        sig = 1.0 / (1.0 + jnp.exp(-pre))
        act_ref[rows, :] = (total * sig * (1.0 + pre * (1.0 - sig))).astype(jnp.bfloat16)

    product_over_channels(-1, side, own_ref, oth_ref, w_ref, y_ref, finish)


NT = (((1,), (1,)), ((), ()))
TN = (((0,), (0,)), ((), ()))


def weight_kernel(sign, side, own_ref, oth_ref, far_own_ref, far_oth_ref, cols_ref, grad_ref):
    held = own_ref.shape[0]
    third = 9 * held
    half = third // 2

    @pl.loop(0, held // ROWS)
    def _(k):
        base = pl.multiple_of(k * ROWS, ROWS)
        for j, ref in enumerate((own_ref, oth_ref)):
            values = ref[pl.ds(base, ROWS), :].astype(jnp.float32)
            for t, (dy, dx) in enumerate(offsets(sign)):
                cols_ref[pl.ds(base + (j * 9 + t) * held, ROWS), :] = shifted(values, dy, dx, side).astype(jnp.bfloat16)

    mine = pl.multiple_of(lax.axis_index("spatial") * half, half)

    @pl.loop(0, far_own_ref.shape[0] // LANES)
    def _(n):
        rows = pl.ds(pl.multiple_of(n * LANES, LANES), LANES)
        far_own, far_oth = far_own_ref[rows, :], far_oth_ref[rows, :]
        grad_ref[:third, rows] = lax.dot_general(
            cols_ref[third:, :], far_own, NT, preferred_element_type=jnp.float32
        ).astype(jnp.bfloat16)
        grad_ref[third:, rows] = (
            lax.dot_general(cols_ref[pl.ds(mine, half), :], far_own, NT, preferred_element_type=jnp.float32)
            + lax.dot_general(cols_ref[pl.ds(third + mine, half), :], far_oth, NT, preferred_element_type=jnp.float32)
        ).astype(jnp.bfloat16)


def mix_kernel(sign, cols_ref, w_ref, out_ref):
    third = w_ref.shape[0] // 3
    away = pl.multiple_of(other_tap(sign) * third, third)

    @pl.loop(0, out_ref.shape[0] // LANES)
    def _(n):
        rows = pl.ds(pl.multiple_of(n * LANES, LANES), LANES)
        out_ref[rows, :] = (
            lax.dot_general(w_ref[third : 2 * third, rows], cols_ref[:third, :], TN, preferred_element_type=jnp.float32)
            + lax.dot_general(w_ref[pl.ds(away, third), rows], cols_ref[third:, :], TN, preferred_element_type=jnp.float32)
        ).astype(jnp.bfloat16)


def call(kernel, outs, scratch, flops, moved, *args):
    vmem = pl.BlockSpec(memory_space=pltpu.VMEM)
    return pl.pallas_call(
        kernel,
        out_shape=outs,
        in_specs=[vmem] * len(args),
        out_specs=jax.tree.map(lambda _: vmem, outs),
        scratch_shapes=scratch,
        cost_estimate=pl.CostEstimate(flops=flops, bytes_accessed=moved, transcendentals=0),
        compiler_params=pltpu.CompilerParams(vmem_limit_bytes=32 * 1024 * 1024),
    )(*args)


def swap(values):
    return lax.ppermute(values, "spatial", [(0, 1), (1, 0)])


def total_over_samples(part):
    return lax.psum(part, "samples")


def joined(mine, theirs, sign, held):
    third = 9 * held
    first = lax.axis_index("spatial") == 0
    zero = jnp.where(first, mine, theirs)
    one = jnp.where(first, theirs, mine)
    low, high = (one, zero) if sign > 0 else (zero, one)
    whole = jnp.concatenate([low[:third], zero[third:], one[third:], high[:third]], axis=0)
    return whole.astype(jnp.float32).reshape(27, held, whole.shape[1])


def body(features, conv_one, conv_two, cotangent):
    held, plane = features.shape[0], features.shape[3]
    full = conv_one.shape[2]
    side = math.isqrt(plane)
    third = 9 * held
    f32, b16 = jnp.float32, jnp.bfloat16
    flat = lambda v: v.reshape(held, plane)
    w_one, w_two = conv_one.reshape(27 * held, full), conv_two.reshape(27 * held, full)
    gather = lambda v: lax.all_gather(v, "channel", axis=0, tiled=True)
    work = 2 * 2 * third * full * plane
    small = 6 * held * full

    x = gather(flat(features))
    c = gather(flat(cotangent))
    x_oth, c_oth = swap(x), swap(c)
    y_scratch = [pltpu.VMEM((third, plane), f32)]
    pre, hid = call(
        functools.partial(forward_kernel, side),
        (jax.ShapeDtypeStruct((held, plane), f32), jax.ShapeDtypeStruct((held, plane), b16)),
        y_scratch, work, small, x, x_oth, w_one,
    )
    hid_oth = swap(hid)
    act = call(
        functools.partial(backward_kernel, side),
        jax.ShapeDtypeStruct((held, plane), b16),
        y_scratch, work, small, c, c_oth, w_two, pre,
    )
    act_oth = swap(act)
    grads = lambda sign, own, oth, far, far_oth: call(
        functools.partial(weight_kernel, sign, side),
        (jax.ShapeDtypeStruct((2 * third, plane), b16), jax.ShapeDtypeStruct((third + third // 2, full), b16)),
        [], work, small, own, oth, far, far_oth,
    )
    mix = lambda sign, cols, w: call(
        functools.partial(mix_kernel, sign),
        jax.ShapeDtypeStruct((full, plane), b16),
        [], work, small, cols, w,
    )
    scatter = lambda v: lax.psum_scatter(v, "channel", scatter_dimension=0, tiled=True)
    cols_h, part_two = grads(1, hid, hid_oth, c, c_oth)
    sum_two = total_over_samples(part_two)
    cols_g, part_one = grads(-1, act, act_oth, x, x_oth)
    sum_one = total_over_samples(part_one)
    mixed = scatter(mix(1, cols_h, w_two)).reshape(features.shape)
    input_grad = scatter(mix(-1, cols_g, w_one)).reshape(features.shape)
    grad_two = joined(sum_two, swap(sum_two), 1, held)
    grad_one = joined(sum_one, swap(sum_one), -1, held)
    return mixed, input_grad, grad_one, grad_two


def solution(mesh):
    act = P("channel", "samples", "spatial", None)
    ker = P(None, "channel", None)
    return jax.shard_map(
        body,
        mesh=mesh,
        in_specs=(act, ker, ker, act),
        out_specs=(act, act, ker, ker),
        check_vma=False,
    )
```

time: 416 us -> 260 us (0.62)
  matrix products: 66 us -> 0 us
  waiting for transfers between devices: 233 us -> 186 us
  local copies, waits for them, and re-layouts: 60.9 us -> 20.6 us
  Pallas kernels: 0 us -> 27.3 us
  starting transfers between devices: 16.6 us -> 1.38 us
  other arithmetic: 21.5 us -> 10.4 us
    conv_general_dilated x6 -> x0, matrix products: 66 us -> none  [the longest x2 35.9 us: weight_grad(): lax.conv_general_dilated(padded, upstream, (1, 1, 1), [(0, 0), (0, 0), (0...]
    all_gather x2, waiting for transfers between devices: 88.4 us -> 60.5 us  [body(): gather = lambda v: lax.all_gather(v, 'channel', axis=0, tiled=True)]
    pallas_call x0 -> x6, Pallas kernels: none -> 27.3 us  [call(): pl.pallas_call(kernel, out_shape=outs, in_specs=[vmem] * len(args), out_s...]
    psum x1, waiting for transfers between devices: 104 us -> 86.6 us  [total_over_samples(): return lax.psum(part, 'samples')]
    ppermute x8 -> x6, starting transfers between devices: 16.4 us -> 1.19 us  [swap(): return lax.ppermute(values, 'spatial', [(0, 1), (1, 0)])]
    conv_general_dilated x11 -> x0, local copies, waits for them, and re-layouts: 10.6 us -> none  [the longest x7 7.43 us: forward_conv(): lax.conv_general_dilated(source, as_taps(kernel), (1, 1, 1), [(0, 0), (1,...]
    reshape x5 -> x0, local copies, waits for them, and re-layouts: 8.91 us -> none  [to_grid(): values.reshape(values.shape[0], values.shape[1], values.shape[2], SIDE, S...]
    concatenate x4 -> x2, other arithmetic: 8.5 us -> 0.54 us  [joined(): jnp.concatenate([low[:third], zero[third:], one[third:], high[:third]], a...]
  transfers between devices with their start and end apart: 13 -> 11, of which waited for: 6 -> 5; matrix products, arithmetic and copies ran while one was open for 32% -> 4% of each run, Pallas kernels for 0% -> 9%
where the time goes in v1:
time: 260 us
  waiting for transfers between devices  186 us (72%)
  Pallas kernels  27.3 us (10%)
  local copies, waits for them, and re-layouts  20.6 us (8%)
  between operations  14 us (5%)
  other arithmetic  10.4 us (4%)
    psum x1, waiting for transfers between devices, total_over_samples(): return lax.psum(part, 'samples')  86.6 us
    all_gather x2, waiting for transfers between devices, body(): gather = lambda v: lax.all_gather(v, 'channel', axis=0, tiled=True)  60.5 us
    reduce_scatter x2, waiting for transfers between devices, body(): lax.psum_scatter(v, 'channel', scatter_dimension=0, tiled=True)  37.4 us
    pallas_call x6, Pallas kernels, call(): pl.pallas_call(kernel, out_shape=outs, in_specs=[vmem] * len(args), out_s...  27.3 us
    unnamed x34, local copies, waits for them, and re-layouts  20.3 us
    convert_element_type x2, other arithmetic, joined(): return whole.astype(jnp.float32).reshape(27, held, whole.shape[1])  7.93 us
  transfers between devices with their start and end apart: 11, of which 5 were waited for; matrix products, arithmetic and copies ran while one was open for 4% of the time, Pallas kernels for 9%

profile of v1, /device:TPU:0, one launch (start us, length us, event | category | flops | bytes accessed | tf_op | source)
XLA Modules:
  0.0 259.6 jit_solution(14240829170843163944)
XLA Ops:
  7.2 0.0 all-gather.5.cloned.1.call-start
  7.2 0.7 all-gather.5.cloned.1.call-update
  7.9 0.0 all-gather.7.cloned.1.call-start
  7.9 0.7 all-gather.7.cloned.1.call-update
  8.6 0.0 all-reduce.3.cloned.1.call-start
  8.7 31.6 %all-gather.5.cloned.1.call-done = bf16[512,1,1,1024]{3,0,2,1:T(8,128)(2,1)} async-done(((bf16[128,1,1,1024]{3,0,2,1:T(8,128)(2,1)}), bf16[512,1,1,1024]{3,0,2,1:T(8,128)(2,1)}) %all-gather.5.cloned.1.call-update) | async-done | bytes 1048592 | tf_op jit(solution)/shard_map/all_gather | solution.py:161
  40.3 29.0 %all-gather.7.cloned.1.call-done = bf16[512,1,1,1024]{3,0,2,1:T(8,128)(2,1)} async-done(((bf16[128,1,1,1024]{3,0,2,1:T(8,128)(2,1)}), bf16[512,1,1,1024]{3,0,2,1:T(8,128)(2,1)}) %all-gather.7.cloned.1.call-update) | async-done | bytes 1048592 | tf_op jit(solution)/shard_map/all_gather | solution.py:161
  69.2 1.0 copy-done.12
  70.2 2.0 copy-done.5
  72.2 1.2 copy-done.9
  73.4 1.2 copy-done.13
  74.7 5.0 %shard_map.75 = (f32[128,1024]{1,0:T(8,128)S(1)}, bf16[128,1024]{1,0:T(8,128)(2,1)S(1)}) custom-call(bf16[512,1024]{1,0:T(8,128)(2,1)S(1)} %bitcast.15, bf16[512,1024]{1,0:T(8,128)(2,1)S(1)} %copy-done.13, bf16[3456,512]{1,0:T(8,128)(2,1)S(1)} %bitcast.12), custom_call_target="tpu_custom_call" | custom-call | flops 2415919104 | bytes 393216 | tf_op jit(solution)/shard_map/pallas_call | solution.py:124
  79.6 0.6 collective-permute-start.1
  80.2 4.9 %shard_map.78.own_ref = bf16[128,1024]{1,0:T(8,128)(2,1)S(1)} custom-call(bf16[512,1024]{1,0:T(8,128)(2,1)S(1)} %bitcast.18, bf16[512,1024]{1,0:T(8,128)(2,1)S(1)} %collective-permute-done.2.far_oth_ref.oth_ref, bf16[3456,512]{1,0:T(8,128)(2,1)S(1)} %bitcast.10, f32[128,1024]{1,0:T(8,128)S(1)} %get-tuple-element.12.pre_ref), custom_call_target="tpu_custom_call" | custom-call | flops 2415919104 | bytes 393216 | tf_op jit(solution)/shard_map/pallas_call | solution.py:124
  85.1 0.0 copy-start.14
  85.1 0.1 collective-permute-start.3
  85.2 4.6 %shard_map.76 = (bf16[2304,1024]{1,0:T(8,128)(2,1)S(1)}, bf16[1728,512]{1,0:T(8,128)(2,1)S(1)}) custom-call(bf16[128,1024]{1,0:T(8,128)(2,1)S(1)} %get-tuple-element.10.own_ref, bf16[128,1024]{1,0:T(8,128)(2,1)S(1)} %collective-permute-done.1.oth_ref, bf16[512,1024]{1,0:T(8,128)(2,1)S(1)} %bitcast.19, ...), custom_call_target="tpu_custom_call" | custom-call | flops 2415919104 | bytes 393216 | tf_op jit(solution)/shard_map/pallas_call | solution.py:124
  89.8 0.0 copy-start.2
  89.8 2.2 copy-done.2
  92.0 1.2 copy-done.7
  93.2 4.6 %shard_map.79 = (bf16[2304,1024]{1,0:T(8,128)(2,1)S(1)}, bf16[1728,512]{1,0:T(8,128)(2,1)S(1)}) custom-call(bf16[128,1024]{1,0:T(8,128)(2,1)S(1)} %shard_map.78.own_ref, bf16[128,1024]{1,0:T(8,128)(2,1)S(1)} %collective-permute-done.3.oth_ref, bf16[512,1024]{1,0:T(8,128)(2,1)S(1)} %bitcast.16, bf16[512,1024]{1,0:T(8,128)(2,1)S(1)} %copy-done.14), custom_call_target="tpu_custom_call" | custom-call | flops 2415919104 | bytes 393216 | tf_op jit(solution)/shard_map/pallas_call | solution.py:124
  97.8 0.0 copy-start
  97.8 2.2 copy-done
  100.0 1.2 copy-done.8
  101.2 0.0 all-reduce.3.cloned.1.call-update
  101.3 0.0 reduce-scatter.3.cloned.1.call-start
  101.3 2.3 copy-done.3
  103.7 4.2 %shard_map.77 = bf16[512,1024]{1,0:T(8,128)(2,1)} custom-call(bf16[2304,1024]{1,0:T(8,128)(2,1)S(1)} %copy-done.3, bf16[3456,512]{1,0:T(8,128)(2,1)S(1)} %bitcast.11), custom_call_target="tpu_custom_call" | custom-call | flops 2415919104 | bytes 393216 | tf_op jit(solution)/shard_map/pallas_call | solution.py:124
  107.8 0.0 reduce-scatter.3.cloned.1.call-update
  107.9 0.0 reduce-scatter.5.cloned.1.call-start
  107.9 86.6 %all-reduce.3.cloned.1.call-done = (bf16[1728,512]{1,0:T(8,128)(2,1)}, bf16[1728,512]{1,0:T(8,128)(2,1)}) async-done(((bf16[1728,512]{1,0:T(8,128)(2,1)}, bf16[1728,512]{1,0:T(8,128)(2,1)}), (bf16[1728,512]{1,0:T(8,128)(2,1)}, bf16[1728,512]{1,0:T(8,128)(2,1)})) %all-reduce.3.cloned.1.call-update) | async-done | bytes 3538960 | tf_op jit(solution)/shard_map/psum | solution.py:140
  194.5 0.5 collective-permute-start.5
  195.0 2.3 copy-done.1
  197.3 2.0 copy-done.6
  199.3 4.1 %shard_map.80 = bf16[512,1024]{1,0:T(8,128)(2,1)} custom-call(bf16[2304,1024]{1,0:T(8,128)(2,1)S(1)} %copy-done.1, bf16[3456,512]{1,0:T(8,128)(2,1)S(1)} %bitcast.13), custom_call_target="tpu_custom_call" | custom-call | flops 2415919104 | bytes 393216 | tf_op jit(solution)/shard_map/pallas_call | solution.py:124
  203.4 0.0 reduce-scatter.5.cloned.1.call-update
  203.5 1.7 broadcast_select_fusion.3
  205.3 0.1 slice.28
  205.4 1.3 copy-done.15
  206.7 0.2 broadcast_select_fusion.1
  207.0 0.1 slice.29
  207.1 0.1 slice.32
  207.2 0.3 pad_maximum_fusion.1
  207.5 4.0 %convert.3 = f32[27,128,512]{2,1,0:T(8,128)} convert(bf16[27,128,512]{2,1,0:T(8,128)(2,1)S(1)} %bitcast.20) | non-fusion elementwise | flops 1769472 | bytes 10616832 | tf_op jit(solution)/shard_map/convert_element_type | solution.py:150
  211.4 0.3 pad_maximum_fusion
  211.7 4.0 %convert.2 = f32[27,128,512]{2,1,0:T(8,128)} convert(bf16[27,128,512]{2,1,0:T(8,128)(2,1)S(1)} %bitcast.21) | non-fusion elementwise | flops 1769472 | bytes 10616832 | tf_op jit(solution)/shard_map/convert_element_type | solution.py:150
  215.7 8.8 %reduce-scatter.3.cloned.1.call-done = bf16[128,1024]{1,0:T(8,128)(2,1)} async-done(((bf16[512,1024]{1,0:T(8,128)(2,1)}), bf16[128,1024]{1,0:T(8,128)(2,1)}) %reduce-scatter.3.cloned.1.call-update) | async-done | bytes 262160 | tf_op jit(solution)/shard_map/reduce_scatter | solution.py:191
  224.5 28.6 %reduce-scatter.5.cloned.1.call-done = bf16[128,1024]{1,0:T(8,128)(2,1)} async-done(((bf16[512,1024]{1,0:T(8,128)(2,1)}), bf16[128,1024]{1,0:T(8,128)(2,1)}) %reduce-scatter.5.cloned.1.call-update) | async-done | bytes 262160 | tf_op jit(solution)/shard_map/reduce_scatter | solution.py:191
  (31 shorter events, 0.2 us)
Async XLA Ops:
  7.2 33.1 %all-gather.5.cloned.1.call-start = ((), (), s32[]{:S(2)}) async-start(), calls=%async_computation.4 | async-start | bytes 1310720 | tf_op jit(solution)/shard_map/all_gather | solution.py:161
  7.9 61.3 %all-gather.7.cloned.1.call-start = ((), (), s32[]{:S(2)}) async-start(), calls=%async_computation.5 | async-start | bytes 1310720 | tf_op jit(solution)/shard_map/all_gather | solution.py:161
  8.6 185.8 %all-reduce.3.cloned.1.call-start = ((), (), s32[]{:S(2)}) async-start(), calls=%async_computation.6 | async-start | bytes 7077888 | tf_op jit(solution)/shard_map/psum | solution.py:140
  40.3 29.0 %collective-permute-start = (bf16[512,1024]{1,0:T(8,128)(2,1)}, bf16[512,1024]{1,0:T(8,128)(2,1)S(1)}, u32[]{:S(2)}, u32[]{:S(2)}) collective-permute-start(bf16[512,1024]{1,0:T(8,128)(2,1)} %bitcast.14), channel_id=1, source_target_pairs={{0,1},{1,0},{2,3},{3,2},{4,5},{5,4},{6,7},{7,6},{8,9},{9,8},{10,11... | collective-permute-start | bytes 3145736 | tf_op jit(solution)/shard_map/ppermute | solution.py:136
  69.2 11.0 %collective-permute-start.2 = (bf16[512,1024]{1,0:T(8,128)(2,1)}, bf16[512,1024]{1,0:T(8,128)(2,1)S(1)}, u32[]{:S(2)}, u32[]{:S(2)}) collective-permute-start(bf16[512,1024]{1,0:T(8,128)(2,1)} %bitcast.17), channel_id=1, source_target_pairs={{0,1},{1,0},{2,3},{3,2},{4,5},{5,4},{6,7},{7,6},{8,9},{9,8},{10,11... | collective-permute-start | bytes 3145736 | tf_op jit(solution)/shard_map/ppermute | solution.py:136
  69.2 1.0 copy-start.12
  70.2 2.0 copy-start.5
  72.2 1.2 copy-start.9
  73.4 1.2 copy-start.13
  74.7 5.6 %copy-start.4 = (bf16[27,128,512]{2,1,0:T(8,128)(2,1)S(1)}, bf16[27,128,512]{2,1,0:T(8,128)(2,1)}, u32[]{:S(2)}) copy-start(bf16[27,128,512]{2,1,0:T(8,128)(2,1)} %param.6) | copy-start | bytes 10616836
  74.7 5.6 %copy-start.11 = (bf16[512,1,1,1024]{3,0,2,1:T(8,128)(2,1)S(1)}, bf16[512,1,1,1024]{3,0,2,1:T(8,128)(2,1)}, u32[]{:S(2)}) copy-start(bf16[512,1,1,1024]{3,0,2,1:T(8,128)(2,1)} %all-gather.7.cloned.1.call-done) | copy-start | bytes 3145732
  79.6 5.6 %collective-permute-start.1 = (bf16[128,1024]{1,0:T(8,128)(2,1)S(1)}, bf16[128,1024]{1,0:T(8,128)(2,1)S(1)}, u32[]{:S(2)}, u32[]{:S(2)}) collective-permute-start(bf16[128,1024]{1,0:T(8,128)(2,1)S(1)} %get-tuple-element.10.own_ref), channel_id=1, source_target_pairs={{0,1},{1,0},{2,3},{3,2},{4,5},{5,4},{6,7},{7,6},{8,9},{9,8},{10,11... | collective-permute-start | bytes 786440 | tf_op jit(solution)/shard_map/ppermute | solution.py:136
  85.1 8.1 %copy-start.10 = (bf16[512,1,1,1024]{3,0,2,1:T(8,128)(2,1)S(1)}, bf16[512,1,1,1024]{3,0,2,1:T(8,128)(2,1)}, u32[]{:S(2)}) copy-start(bf16[512,1,1,1024]{3,0,2,1:T(8,128)(2,1)} %all-gather.5.cloned.1.call-done) | copy-start | bytes 3145732
  85.1 8.1 %copy-start.14 = (bf16[512,1024]{1,0:T(8,128)(2,1)S(1)}, bf16[512,1024]{1,0:T(8,128)(2,1)}, u32[]{:S(2)}) copy-start(bf16[512,1024]{1,0:T(8,128)(2,1)} %copy-done.12) | copy-start | bytes 3145732
  85.1 8.1 %collective-permute-start.3 = (bf16[128,1024]{1,0:T(8,128)(2,1)S(1)}, bf16[128,1024]{1,0:T(8,128)(2,1)S(1)}, u32[]{:S(2)}, u32[]{:S(2)}) collective-permute-start(bf16[128,1024]{1,0:T(8,128)(2,1)S(1)} %shard_map.78.own_ref), channel_id=1, source_target_pairs={{0,1},{1,0},{2,3},{3,2},{4,5},{5,4},{6,7},{7,6},{8,9},{9,8},{10,11... | collective-permute-start | bytes 786440 | tf_op jit(solution)/shard_map/ppermute | solution.py:136
  89.8 2.2 copy-start.2
  92.0 1.2 copy-start.7
  97.8 2.2 copy-start
  100.0 1.2 copy-start.8
  101.3 123.2 %reduce-scatter.3.cloned.1.call-start = ((), (), s32[]{:S(2)}) async-start(), calls=%async_computation.2 | async-start | bytes 1310720 | tf_op jit(solution)/shard_map/reduce_scatter | solution.py:191
  101.3 2.3 copy-start.3
  107.9 145.2 %reduce-scatter.5.cloned.1.call-start = ((), (), s32[]{:S(2)}) async-start(), calls=%async_computation.3 | async-start | bytes 1310720 | tf_op jit(solution)/shard_map/reduce_scatter | solution.py:191
  194.5 9.0 %collective-permute-start.4 = (bf16[1728,512]{1,0:T(8,128)(2,1)}, bf16[1728,512]{1,0:T(8,128)(2,1)}, u32[]{:S(2)}, u32[]{:S(2)}) collective-permute-start(bf16[1728,512]{1,0:T(8,128)(2,1)} %get-tuple-element.16), channel_id=1, source_target_pairs={{0,1},{1,0},{2,3},{3,2},{4,5},{5,4},{6,7},{7,6},{8,9},{9,8},{10,11... | collective-permute-start | bytes 5308424 | tf_op jit(solution)/shard_map/ppermute | solution.py:136
  194.5 10.9 %collective-permute-start.5 = (bf16[1728,512]{1,0:T(8,128)(2,1)}, bf16[1728,512]{1,0:T(8,128)(2,1)S(1)}, u32[]{:S(2)}, u32[]{:S(2)}) collective-permute-start(bf16[1728,512]{1,0:T(8,128)(2,1)} %get-tuple-element.17), channel_id=1, source_target_pairs={{0,1},{1,0},{2,3},{3,2},{4,5},{5,4},{6,7},{7,6},{8,9},{9,8},{10,11... | collective-permute-start | bytes 5308424 | tf_op jit(solution)/shard_map/ppermute | solution.py:136
  195.0 2.3 copy-start.1
  197.3 2.0 copy-start.6
  199.3 4.2 %copy-start.16 = (bf16[1728,512]{1,0:T(8,128)(2,1)S(1)}, bf16[1728,512]{1,0:T(8,128)(2,1)}, u32[]{:S(2)}) copy-start(bf16[1728,512]{1,0:T(8,128)(2,1)} %get-tuple-element.16) | copy-start | bytes 5308420
  205.2 1.5 copy-start.15
Sparse Core Ops, SparseCore 0:
  9.5 30.6 all-gather.4
  41.8 27.3 all-gather.6
  101.4 93.0 all-reduce.2
  197.2 27.2 reduce-scatter.2
  227.2 25.7 reduce-scatter.4
